TPU v7x, 128 devices: a whole 4x4x4 slice. The times are simulated.
128 devices in a mesh: row: 8 (over z_lo, y), col: 16 (over z_hi, x, core).
Axes of the slice: x: 4, y: 4, z: 4 (z_hi: 2, z_lo: 2; z = z_hi * 2 + z_lo), core: 2. Of those that a mesh axis runs over, the one named last changes fastest.
Arguments:
- density: float32 [6144, 6144], P('row', 'col'), may hold values from -1 to 1, as said below
- response: float32 [6144, 6144], P('row', 'col'), may hold values from -1 to 1, as said below
- density_mask: int32 [48, 48], replicated, may hold values from 0 to 1, as said below
- response_mask: int32 [48, 48], replicated, may hold values from 0 to 1, as said below
- branch: int32 [48], replicated, may hold values from 0 to 1
Outputs:
- new_density: float32 [6144, 6144], P('row', 'col')
- new_response: float32 [6144, 6144], P('row', 'col')
Inputs may be any that keep to these rules, and one draw needn't show every extreme that they name: `density`: symmetric: equal to its own transpose. `response`: symmetric: equal to its own transpose. `density_mask`: symmetric, with ones on the diagonal. `response_mask`: symmetric, with ones on the diagonal.
All inputs are finite; a program needn't handle non-finite values.
Results may differ from a plain program's by a relative error of at most 0.000067.
Values sent between devices are 32-bit elements; how exact they have to be, the bound alone decides.
No kernel may reach another device: no remote copies, remote signals or barrier semaphores. Data moves between devices by JAX's collectives and lax.ppermute only.
A program may use at most 192 MiB of HBM per device.

v0:
```python
import jax
import jax.numpy as jnp
from jax import lax
from jax.sharding import PartitionSpec as P

BLOCK = 128
precise = lax.Precision.HIGHEST


def in_one_piece(arrays, axis, dim, along):
    ends, at = ([], 0)
    for a in arrays[:-1]:
        at += a.shape[along]
        ends.append(at)
    both = jnp.concatenate(arrays, axis=along)
    return tuple(jnp.split(lax.all_gather(both, axis, axis=dim, tiled=True), ends, axis=along))


def expand_mask(local_tile, block_mask):
    row_count, col_count = local_tile.shape
    row_blocks = row_count // BLOCK
    col_blocks = col_count // BLOCK
    row_start = lax.axis_index("row") * row_blocks
    col_start = lax.axis_index("col") * col_blocks
    window = lax.dynamic_slice(block_mask, (row_start, col_start), (row_blocks, col_blocks)).astype(
        jnp.float32
    )
    shaped = local_tile.reshape(row_blocks, BLOCK, col_blocks, BLOCK) * window[:, None, :, None]
    return shaped.reshape(row_count, col_count)


def matmul(left, right):
    return jnp.dot(left, right, precision=precise, preferred_element_type=jnp.float32)


def per_device(density, response, density_mask, response_mask, branch):
    masked_density = expand_mask(density, density_mask)
    masked_response = expand_mask(response, response_mask)
    column_density, column_response = (
        lax.all_gather(masked_density, "row", axis=0, tiled=True),
        lax.all_gather(masked_response, "row", axis=0, tiled=True),
    )
    segments = in_one_piece((masked_density, masked_response), "col", 1, 0)
    square = matmul(segments[0], column_density)
    product = matmul(segments[0], column_response)
    reversed_tile = matmul(segments[1], column_density)
    combined = product + reversed_tile
    local_blocks = density.shape[0] // BLOCK
    block_start = lax.axis_index("row") * local_blocks
    local_branch = lax.dynamic_slice_in_dim(branch, block_start, local_blocks, 0)
    chosen = jnp.repeat(local_branch, BLOCK)[:, None]
    new_density = jnp.where(chosen == 0, square, 2.0 * masked_density - square)
    new_response = jnp.where(chosen == 0, combined, 2.0 * masked_response - combined)
    return (new_density, new_response)


def solution(mesh):
    return jax.shard_map(
        per_device,
        mesh=mesh,
        in_specs=(P("row", "col"), P("row", "col"), P(), P(), P()),
        out_specs=(P("row", "col"), P("row", "col")),
        check_vma=False,
    )
```

profile of v0, /device:TPU:1, one launch (start us, length us, event | category | flops | bytes accessed | tf_op | source)
XLA Modules:
  0.0 463.0 jit_solution(11147713963077403689)
XLA Ops:
  7.2 0.0 all-gather.6.cloned.1.call-start
  7.2 0.8 dynamic-slice_convert_fusion
  8.0 0.1 copy.7
  8.1 0.2 mul.39
  8.3 0.3 copy.16
  8.6 0.0 copy-start.4
  8.6 0.4 copy.8
  8.9 0.9 copy-done.4
  9.8 1.1 mul.41
  11.0 0.0 all-gather.6.cloned.1.call-update
  11.0 0.0 all-gather.4.cloned.1.call-start
  11.0 0.1 copy.9
  11.1 0.2 mul.42
  11.3 0.3 copy.15
  11.6 0.4 copy.10
  11.9 0.0 copy-start.1
  11.9 1.5 mul.44
  13.4 0.0 copy-start.2
  13.4 0.1 copy-done.1
  13.6 1.7 pad_maximum_fusion
  15.2 0.0 copy-done.2
  15.2 0.0 copy-start.5
  15.3 0.0 all-gather.4.cloned.1.call-update
  15.3 0.0 all-gather.8.cloned.1.call-start
  15.3 0.7 all-gather.8.cloned.1.call-update
  16.0 0.0 copy-done.5
  16.0 0.1 dynamic-slice_compare_fusion
  16.1 0.1 broadcast_bitcast_fusion
  16.2 99.8 %all-gather.6.cloned.1.call-done = f32[6144,384]{1,0:T(8,128)} async-done(((f32[768,384]{1,0:T(8,128)}), f32[6144,384]{1,0:T(8,128)}) %all-gather.6.cloned.1.call-update) | async-done | bytes 9437200 | tf_op jit(solution)/shard_map/all_gather | solution.py:40
  115.9 205.9 %all-gather.4.cloned.1.call-done = f32[1536,6144]{1,0:T(8,128)} async-done(((f32[1536,384]{1,0:T(8,128)}), f32[1536,6144]{1,0:T(8,128)}) %all-gather.4.cloned.1.call-update) | async-done | bytes 37748752 | tf_op jit(solution)/shard_map/all_gather | solution.py:16
  321.9 0.0 copy-start
  321.9 34.6 %fusion = f32[768,384]{1,0:T(8,128)S(1)} fusion(f32[6144,384]{1,0:T(8,128)} %all-gather.6.cloned.1.call-done, f32[1536,6144]{1,0:T(8,128)} %all-gather.4.cloned.1.call-done), kind=kOutput, calls=%fused_computation | convolution fusion | flops 21743271936 | bytes 29491200 | tf_op jit(solution)/shard_map/dot_general | solution.py:33
  356.5 0.0 copy-done
  356.5 0.0 copy-start.3
  356.5 41.1 %subtract_select_fusion.1 = f32[768,384]{1,0:T(8,128)} fusion(f32[6144,384]{1,0:T(8,128)S(1)} %copy-done, f32[1536,6144]{1,0:T(8,128)} %all-gather.4.cloned.1.call-done, f32[768,384]{1,0:T(8,128)S(1)} %copy-done.1, pred[768]{0:T(1024)(128)(4,1)S(1)} %broadcast_bitcast_fusion), kind=kOutput, calls=%fused_computation.8 | convolution fusion | flops 21744156672 | bytes 30671616 | tf_op jit(solution)/shard_map/dot_general | solution.py:33
  397.6 24.5 %all-gather.8.cloned.1.call-done = f32[6144,384]{1,0:T(8,128)} async-done(((f32[768,384]{1,0:T(8,128)}), f32[6144,384]{1,0:T(8,128)}) %all-gather.8.cloned.1.call-update) | async-done | bytes 9437200 | tf_op jit(solution)/shard_map/all_gather | solution.py:41
  422.2 0.0 copy-done.3
  422.2 34.3 %subtract_select_fusion = f32[768,384]{1,0:T(8,128)} fusion(f32[768,384]{1,0:T(8,128)S(1)} %fusion, f32[6144,384]{1,0:T(8,128)} %all-gather.8.cloned.1.call-done, f32[1536,6144]{1,0:T(8,128)} %all-gather.4.cloned.1.call-done, f32[768,384]{1,0:T(8,128)S(1)} %copy-done.3, pred[768]{0:T(1024)(128)(4,1)S(1)} %broadcast_bitcast_fusion), kind=kOutput, calls=%fused_computation.7 | convolution fusion | flops 21744451584 | bytes 31851264 | tf_op jit(solution)/shard_map/dot_general | solution.py:33
Async XLA Ops:
  7.2 108.8 %all-gather.6.cloned.1.call-start = ((), (), s32[]{:S(2)}) async-start(), calls=%async_computation.1 | async-start | bytes 10616832 | tf_op jit(solution)/shard_map/all_gather | solution.py:40
  8.6 1.3 copy-start.4
  11.0 310.9 %all-gather.4.cloned.1.call-start = ((), (), s32[]{:S(2)}) async-start(), calls=%async_computation | async-start | bytes 40108032 | tf_op jit(solution)/shard_map/all_gather | solution.py:16
  11.9 1.6 copy-start.1
  13.4 1.8 copy-start.2
  15.2 0.8 copy-start.5
  15.3 406.9 %all-gather.8.cloned.1.call-start = ((), (), s32[]{:S(2)}) async-start(), calls=%async_computation.2 | async-start | bytes 10616832 | tf_op jit(solution)/shard_map/all_gather | solution.py:41
  321.9 34.6 %copy-start = (f32[6144,384]{1,0:T(8,128)S(1)}, f32[6144,384]{1,0:T(8,128)}, u32[]{:S(2)}) copy-start(f32[6144,384]{1,0:T(8,128)} %all-gather.6.cloned.1.call-done) | copy-start | bytes 28311556
  356.5 65.7 %copy-start.3 = (f32[768,384]{1,0:T(8,128)S(1)}, f32[768,384]{1,0:T(8,128)}, u32[]{:S(2)}) copy-start(f32[768,384]{1,0:T(8,128)} %copy-done.2) | copy-start | bytes 3538948
Sparse Core Ops, SparseCore 0:
  11.1 104.7 all-gather.5
  118.4 203.4 all-gather.3
  323.5 98.6 all-gather.7
where the time goes:
time: 463 us
  waiting for transfers between devices  331 us (71%)
  matrix products  110 us (24%)
  between operations  13.9 us (3%)
  other arithmetic  5.18 us (1%)
    all_gather x1, waiting for transfers between devices, in_one_piece(): lax.all_gather(both, axis, axis=dim, tiled=True)  206 us
    dot_general x3, matrix products, matmul(): jnp.dot(left, right, precision=precise, preferred_element_type=jnp.float32)  110 us
    all_gather x1, waiting for transfers between devices, per_device(): lax.all_gather(masked_density, 'row', axis=0, tiled=True)  99.8 us
    all_gather x1, waiting for transfers between devices, per_device(): lax.all_gather(masked_response, 'row', axis=0, tiled=True)  24.5 us
  transfers between devices with their start and end apart: 3, of which 3 were waited for; matrix products, arithmetic and copies ran while one was open for 17% of the time, Pallas kernels for 0%

commit v1 on v0

--- a/solution.py
+++ b/solution.py
@@ -5,6 +5,11 @@
 
 BLOCK = 128
 precise = lax.Precision.HIGHEST
+
+
+def exchange_gather(block, name, along):
+    sent = jnp.stack([block] * lax.axis_size(name))
+    return jnp.concatenate(lax.all_to_all(sent, name, 0, 0), axis=along)
 
 
 def in_one_piece(arrays, axis, dim, along):
@@ -37,7 +42,7 @@
     masked_density = expand_mask(density, density_mask)
     masked_response = expand_mask(response, response_mask)
     column_density, column_response = (
-        lax.all_gather(masked_density, "row", axis=0, tiled=True),
+        exchange_gather(masked_density, "row", 0),
         lax.all_gather(masked_response, "row", axis=0, tiled=True),
     )
     segments = in_one_piece((masked_density, masked_response), "col", 1, 0)

time: 463 us -> 461 us (level)
  matrix products: 110 us -> 102 us
  starting transfers between devices: 0.12 us -> 6.57 us
    all_to_all x0 -> x1, waiting for transfers between devices: none -> 122 us  [exchange_gather(): return jnp.concatenate(lax.all_to_all(sent, name, 0, 0), axis=along)]
    all_gather x1 -> x0, waiting for transfers between devices: 99.8 us -> none  [per_device(): lax.all_gather(masked_density, 'row', axis=0, tiled=True)]
    all_gather x1, waiting for transfers between devices: 206 us -> 172 us  [in_one_piece(): lax.all_gather(both, axis, axis=dim, tiled=True)]
    all_gather x1, waiting for transfers between devices: 24.5 us -> 33.3 us  [per_device(): lax.all_gather(masked_response, 'row', axis=0, tiled=True)]
    dot_general x3, matrix products: 110 us -> 102 us  [matmul(): jnp.dot(left, right, precision=precise, preferred_element_type=jnp.float32)]
    all_to_all x0 -> x1, starting transfers between devices: none -> 6.5 us  [exchange_gather(): return jnp.concatenate(lax.all_to_all(sent, name, 0, 0), axis=along)]
  transfers between devices with their start and end apart: 3 -> 3, of which waited for: 3 -> 3; matrix products, arithmetic and copies ran while one was open for 17% -> 16% of each run, Pallas kernels for 0% -> 0%
where the time goes in v1:
time: 461 us
  waiting for transfers between devices  328 us (71%)
  matrix products  102 us (22%)
  between operations  14.1 us (3%)
  starting transfers between devices  6.57 us (1%)
  local copies, waits for them, and re-layouts  6.22 us (1%)
    all_gather x1, waiting for transfers between devices, in_one_piece(): lax.all_gather(both, axis, axis=dim, tiled=True)  172 us
    all_to_all x1, waiting for transfers between devices, exchange_gather(): return jnp.concatenate(lax.all_to_all(sent, name, 0, 0), axis=along)  122 us
    dot_general x3, matrix products, matmul(): jnp.dot(left, right, precision=precise, preferred_element_type=jnp.float32)  102 us
    all_gather x1, waiting for transfers between devices, per_device(): lax.all_gather(masked_response, 'row', axis=0, tiled=True)  33.3 us
  transfers between devices with their start and end apart: 3, of which 3 were waited for; matrix products, arithmetic and copies ran while one was open for 16% of the time, Pallas kernels for 0%

profile of v1, /device:TPU:1, one launch (start us, length us, event | category | flops | bytes accessed | tf_op | source)
XLA Modules:
  0.0 460.8 jit_solution(14790313708173095497)
XLA Ops:
  7.2 0.0 all-gather.3.cloned.1.call-start
  7.2 0.8 dynamic-slice_convert_fusion
  8.0 0.1 copy.7
  8.1 0.2 mul.41
  8.3 0.3 copy.16
  8.6 0.4 copy.8
  8.9 0.1 copy.9
  9.0 0.2 mul.44
  9.2 0.3 copy.15
  9.5 0.4 copy.10
  9.8 0.0 copy-start.2
  9.8 1.5 mul.43
  11.3 0.1 copy-done.2
  11.5 0.1 mul.46
  11.6 0.0 copy-start
  11.6 1.7 pad_maximum_fusion
  13.3 0.0 copy-done
  13.4 0.0 all-gather.3.cloned.1.call-update
  13.4 0.0 all-gather.5.cloned.1.call-start
  13.4 0.7 all-gather.5.cloned.1.call-update
  14.1 4.2 stack.3
  18.3 0.0 copy-start.3
  18.3 6.5 %all-to-all-start = ((f32[8,768,384]{2,1,0:T(8,128)}), f32[8,768,384]{2,1,0:T(8,128)}, u32[]{:S(2)}, u32[]{:S(2)}) async-start(f32[8,768,384]{2,1,0:T(8,128)} %stack.3), calls=%async_computation | async-start | bytes 18874368 | tf_op jit(solution)/shard_map/all_to_all | solution.py:12
  24.8 0.0 copy-done.3
  24.8 0.1 dynamic-slice_compare_fusion
  24.9 0.1 broadcast_bitcast_fusion
  25.0 122.0 %all-to-all-done = f32[8,768,384]{2,1,0:T(8,128)} async-done(((f32[8,768,384]{2,1,0:T(8,128)}), f32[8,768,384]{2,1,0:T(8,128)}, u32[]{:S(2)}, u32[]{:S(2)}) %all-to-all-start) | async-done | bytes 9437216 | tf_op jit(solution)/shard_map/all_to_all | solution.py:12
  147.0 171.7 %all-gather.3.cloned.1.call-done = f32[1536,6144]{1,0:T(8,128)} async-done(((f32[1536,384]{1,0:T(8,128)}), f32[1536,6144]{1,0:T(8,128)}) %all-gather.3.cloned.1.call-update) | async-done | bytes 37748752 | tf_op jit(solution)/shard_map/all_gather | solution.py:21
  318.7 33.1 %fusion = f32[768,384]{1,0:T(8,128)S(1)} fusion(f32[6144,384]{1,0:T(8,128)} %bitcast.1, f32[1536,6144]{1,0:T(8,128)} %all-gather.3.cloned.1.call-done), kind=kOutput, calls=%fused_computation | convolution fusion | flops 21743271936 | bytes 29491200 | tf_op jit(solution)/shard_map/dot_general | solution.py:38
  351.8 0.0 copy-start.1
  351.8 34.5 %subtract_select_fusion.1 = f32[768,384]{1,0:T(8,128)} fusion(f32[6144,384]{1,0:T(8,128)} %bitcast.1, f32[1536,6144]{1,0:T(8,128)} %all-gather.3.cloned.1.call-done, f32[768,384]{1,0:T(8,128)S(1)} %mul.43, pred[768]{0:T(1024)(128)(4,1)S(1)} %broadcast_bitcast_fusion), kind=kOutput, calls=%fused_computation.8 | convolution fusion | flops 21744156672 | bytes 30671616 | tf_op jit(solution)/shard_map/dot_general | solution.py:38
  386.3 33.3 %all-gather.5.cloned.1.call-done = f32[6144,384]{1,0:T(8,128)} async-done(((f32[768,384]{1,0:T(8,128)}), f32[6144,384]{1,0:T(8,128)}) %all-gather.5.cloned.1.call-update) | async-done | bytes 9437200 | tf_op jit(solution)/shard_map/all_gather | solution.py:46
  419.6 0.0 copy-done.1
  419.6 34.3 %subtract_select_fusion = f32[768,384]{1,0:T(8,128)} fusion(f32[768,384]{1,0:T(8,128)S(1)} %fusion, f32[6144,384]{1,0:T(8,128)} %all-gather.5.cloned.1.call-done, f32[1536,6144]{1,0:T(8,128)} %all-gather.3.cloned.1.call-done, f32[768,384]{1,0:T(8,128)S(1)} %copy-done.1, pred[768]{0:T(1024)(128)(4,1)S(1)} %broadcast_bitcast_fusion), kind=kOutput, calls=%fused_computation.7 | convolution fusion | flops 21744451584 | bytes 31851264 | tf_op jit(solution)/shard_map/dot_general | solution.py:38
Async XLA Ops:
  7.2 311.6 %all-gather.3.cloned.1.call-start = ((), (), s32[]{:S(2)}) async-start(), calls=%async_computation.1 | async-start | bytes 40108032 | tf_op jit(solution)/shard_map/all_gather | solution.py:21
  9.8 1.6 copy-start.2
  11.6 1.8 copy-start
  13.4 406.2 %all-gather.5.cloned.1.call-start = ((), (), s32[]{:S(2)}) async-start(), calls=%async_computation.2 | async-start | bytes 10616832 | tf_op jit(solution)/shard_map/all_gather | solution.py:46
  18.3 6.5 %copy-start.3 = (s32[48]{0:T(128)S(1)}, s32[48]{0:T(128)}, u32[]{:S(2)}) copy-start(s32[48]{0:T(128)} %param.9) | copy-start | bytes 580
  18.3 128.7 %all-to-all-start = ((f32[8,768,384]{2,1,0:T(8,128)}), f32[8,768,384]{2,1,0:T(8,128)}, u32[]{:S(2)}, u32[]{:S(2)}) async-start(f32[8,768,384]{2,1,0:T(8,128)} %stack.3), calls=%async_computation | async-start | bytes 18874368 | tf_op jit(solution)/shard_map/all_to_all | solution.py:12
  351.8 67.8 %copy-start.1 = (f32[768,384]{1,0:T(8,128)S(1)}, f32[768,384]{1,0:T(8,128)}, u32[]{:S(2)}) copy-start(f32[768,384]{1,0:T(8,128)} %copy-done) | copy-start | bytes 3538948
Sparse Core Ops, SparseCore 0:
  13.5 305.1 all-gather.2
  320.9 98.6 all-gather.4
